TPU v7x, 32 devices: a whole 2x2x4 slice. The times are simulated.
32 devices in a mesh: dp: 8 (over z, y), hg: 2 (over x), hid: 2 (over core).
Axes of the slice: x: 2, y: 2, z: 4, core: 2. Of those that a mesh axis runs over, the one named last changes fastest.
Arguments:
- tokens: bfloat16 [18816, 768], P(('dp', 'hid')), may hold values from -6 to 6
- big_images: int32 [16], P(('dp', 'hid')), may hold values from 0 to 1, as said below
- norm_gain: bfloat16 [768], replicated, may hold values from 0.5 to 1.5
- w_qkv: bfloat16 [768, 2304], P(None, 'hg'), may hold values from -0.21875 to 0.21875
- qk_gains: bfloat16 [2, 64], replicated, may hold values from 0.099609375 to 1.8984375
- w_out_t: bfloat16 [768, 768], P(None, 'hg'), may hold values from -0.625 to 0.625
- w_in: bfloat16 [768, 3072], P(None, ('hg', 'hid')), may hold values from -0.21875 to 0.21875
- w_back: bfloat16 [768, 3072], P(None, ('hg', 'hid')), may hold values from -0.109375 to 0.109375
- cotangent: bfloat16 [18816, 768], P(('dp', 'hid'), 'hg'), may hold values from -6 to 6
Outputs:
- output: bfloat16 [18816, 768], P(('dp', 'hid'), 'hg')
- token_grad: bfloat16 [18816, 768], P(('dp', 'hid'))
- norm_gain_grad: float32 [768], P(('dp', 'hid'))
- w_qkv_grad: float32 [768, 2304], P(('dp', 'hid'), 'hg')
- qk_gains_grad: float32 [2, 64], replicated
- w_out_t_grad: float32 [768, 768], P(('dp', 'hid'), 'hg')
- w_in_grad: float32 [768, 3072], P('dp', ('hg', 'hid'))
- w_back_grad: float32 [768, 3072], P('dp', ('hg', 'hid'))
Inputs may be any that keep to these rules, and one draw needn't show every extreme that they name: `big_images`: 1 where the 1176 tokens of a group form one image, 0 where they form 6 images of 196 tokens each in order; every draw has groups of both kinds.
All inputs are finite; a program needn't handle non-finite values.
Results may differ from a plain program's by a relative error of at most 0.012.
Values may be sent and summed in bfloat16 or wider, within the bound.
No kernel may reach another device: no remote copies, remote signals or barrier semaphores. Data moves between devices by JAX's collectives and lax.ppermute only.
A program may use at most 256 MiB of HBM per device.

v0:
```python
import jax
import jax.numpy as jnp
from jax import lax
from jax.sharding import PartitionSpec as P

PATCHES = 196


EPSILON = 1e-06


def normalize(values):
    centred = values - jnp.mean(values, axis=-1, keepdims=True)
    inverse = lax.rsqrt(jnp.mean(centred * centred, axis=-1, keepdims=True) + EPSILON)
    return (centred * inverse, inverse)


def normalize_back(upstream, normed, inverse):
    inner = jnp.mean(upstream * normed, axis=-1, keepdims=True)
    return inverse * (upstream - jnp.mean(upstream, axis=-1, keepdims=True) - normed * inner)


def times_t(left, right):
    return lax.dot_general(
        left, right, (((1,), (1,)), ((), ())), preferred_element_type=jnp.float32
    )


def rows_t(left, right):
    return lax.dot_general(
        left, right, (((0,), (0,)), ((), ())), preferred_element_type=jnp.float32
    )


def masked_scores(queries, keys_in, allowed):
    scores = jnp.einsum("gqe,gke->gqk", queries, keys_in, preferred_element_type=jnp.float32)
    return jnp.where(allowed, scores, -1e30)


def head_forward(queries, keys_in, values_in, allowed):
    scores = masked_scores(queries, keys_in, allowed)
    highest = jnp.max(scores, axis=-1, keepdims=True)
    expo_scores = jnp.exp(scores - highest)
    totals = jnp.sum(expo_scores, axis=-1, keepdims=True)
    weights = (expo_scores / totals).astype(jnp.bfloat16)
    attended = jnp.einsum("gqk,gke->gqe", weights, values_in, preferred_element_type=jnp.float32)
    return (attended, (highest + jnp.log(totals))[..., 0])


def head_back(queries, keys_in, values_in, log_total, grad_out, allowed):
    scores = masked_scores(queries, keys_in, allowed)
    probs = jnp.exp(scores - log_total[..., None])
    grad_probs = jnp.einsum("gqe,gke->gqk", grad_out, values_in, preferred_element_type=jnp.float32)
    inner = jnp.sum(grad_probs * probs, axis=-1, keepdims=True)
    grad_scores = (probs * (grad_probs - inner)).astype(jnp.bfloat16)
    grad_values = jnp.einsum(
        "gqk,gqe->gke", probs.astype(jnp.bfloat16), grad_out, preferred_element_type=jnp.float32
    )
    grad_queries = jnp.einsum(
        "gqk,gke->gqe", grad_scores, keys_in, preferred_element_type=jnp.float32
    )
    grad_keys = jnp.einsum("gqk,gqe->gke", grad_scores, queries, preferred_element_type=jnp.float32)
    return (grad_queries, grad_keys, grad_values)


def attention_pass(step_fn, arrays, big_flag):
    heads_here = arrays[0].shape[0]
    tok_rows = arrays[0].shape[1]
    image_of = jnp.arange(tok_rows) // PATCHES
    allowed = (image_of[:, None] == image_of[None, :]) | (big_flag > 0)
    run_allowed = allowed[None]
    shaped = tuple(
        (member.reshape((heads_here, 1, tok_rows // 1) + member.shape[2:]) for member in arrays)
    )
    results = lax.map(lambda blocks: step_fn(*blocks, run_allowed), shaped)
    return tuple((member.reshape((heads_here, tok_rows) + member.shape[3:]) for member in results))


def shards(tokens, big_images, norm_gain, w_qkv, qk_gains, w_out_t, w_in, w_back, cotangent):
    tok_rows = tokens.shape[0]
    width = tokens.shape[1]
    head_size = qk_gains.shape[1]
    heads_here = w_qkv.shape[1] // (3 * head_size)
    half_width = heads_here * head_size
    big_flag = big_images[0]
    head_scale = head_size ** (-0.5)
    inputs = tokens.astype(jnp.float32)
    normed, inverse = normalize(inputs)
    gain_vec = norm_gain.astype(jnp.float32)
    normed_low = (normed * gain_vec).astype(jnp.bfloat16)
    joined = jnp.dot(normed_low, w_qkv, preferred_element_type=jnp.float32).reshape(
        tok_rows, heads_here, 3, head_size
    )
    q_hat, q_inverse = normalize(joined[:, :, 0])
    k_hat, k_inverse = normalize(joined[:, :, 1])
    q_gain = qk_gains[0].astype(jnp.float32)
    k_gain = qk_gains[1].astype(jnp.float32)
    queries = (q_hat * q_gain * head_scale).astype(jnp.bfloat16).transpose(1, 0, 2)
    keys_in = (k_hat * k_gain).astype(jnp.bfloat16).transpose(1, 0, 2)
    values_in = joined[:, :, 2].astype(jnp.bfloat16).transpose(1, 0, 2)
    attended, log_total = attention_pass(head_forward, (queries, keys_in, values_in), big_flag)
    attended_low = attended.astype(jnp.bfloat16).transpose(1, 0, 2).reshape(tok_rows, half_width)
    attn_part = times_t(attended_low, w_out_t)
    normed_all = lax.all_gather(normed_low, "hid", axis=0, tiled=True)
    hidden_pre = jnp.dot(normed_all, w_in, preferred_element_type=jnp.float32)
    hidden_act = jax.nn.gelu(hidden_pre).astype(jnp.bfloat16)
    mlp_part = lax.psum_scatter(
        times_t(hidden_act, w_back).astype(jnp.bfloat16), "hid", scatter_dimension=0, tiled=True
    ).astype(jnp.float32)
    mixed = lax.psum_scatter(attn_part + mlp_part, "hg", scatter_dimension=1, tiled=True)
    out_cols = width // lax.axis_size("hg")
    input_cols = lax.dynamic_slice_in_dim(inputs, lax.axis_index("hg") * out_cols, out_cols, 1)
    output = (input_cols + mixed).astype(jnp.bfloat16)
    grad_out = lax.all_gather(cotangent, "hg", axis=1, tiled=True)
    grad_w_out = rows_t(grad_out, attended_low)
    grad_attended = jnp.dot(grad_out, w_out_t, preferred_element_type=jnp.float32)
    grad_att_low = (
        grad_attended.astype(jnp.bfloat16)
        .reshape(tok_rows, heads_here, head_size)
        .transpose(1, 0, 2)
    )
    grad_queries, grad_keys, grad_values = attention_pass(
        head_back, (queries, keys_in, values_in, log_total, grad_att_low), big_flag
    )
    grad_query = grad_queries.transpose(1, 0, 2) * head_scale
    grad_key = grad_keys.transpose(1, 0, 2)
    qk_partial = jnp.stack(
        [jnp.sum(grad_query * q_hat, axis=(0, 1)), jnp.sum(grad_key * k_hat, axis=(0, 1))]
    )
    grad_q_raw = normalize_back(grad_query * q_gain, q_hat, q_inverse)
    grad_k_raw = normalize_back(grad_key * k_gain, k_hat, k_inverse)
    grad_joined = jnp.stack([grad_q_raw, grad_k_raw, grad_values.transpose(1, 0, 2)], axis=2)
    grad_joined = grad_joined.reshape(tok_rows, 3 * half_width).astype(jnp.bfloat16)
    grad_w_qkv = rows_t(normed_low, grad_joined)
    grad_normed_att = times_t(grad_joined, w_qkv)
    grad_out_all = lax.all_gather(grad_out, "hid", axis=0, tiled=True)
    grad_act = jnp.dot(grad_out_all, w_back, preferred_element_type=jnp.float32)
    grad_up = jax.vjp(jax.nn.gelu, hidden_pre)[1](grad_act)[0].astype(jnp.bfloat16)
    grad_w_back = rows_t(grad_out_all, hidden_act)
    grad_w_in = rows_t(normed_all, grad_up)
    grad_normed_mlp = lax.psum_scatter(
        times_t(grad_up, w_in).astype(jnp.bfloat16), "hid", scatter_dimension=0, tiled=True
    ).astype(jnp.float32)
    grad_normed = lax.psum(grad_normed_att + grad_normed_mlp, "hg")
    token_grad = (
        normalize_back(grad_normed * gain_vec, normed, inverse) + grad_out.astype(jnp.float32)
    ).astype(jnp.bfloat16)
    gain_partial = jnp.sum(grad_normed * normed, axis=0)
    w_qkv_grad, w_out_t_grad, norm_gain_grad = (
        lax.psum_scatter(grad_w_qkv, ("dp", "hid"), scatter_dimension=0, tiled=True),
        lax.psum_scatter(grad_w_out, ("dp", "hid"), scatter_dimension=0, tiled=True),
        lax.psum_scatter(gain_partial, ("dp", "hid"), scatter_dimension=0, tiled=True),
    )
    w_in_grad, w_back_grad = (
        lax.psum_scatter(
            grad_w_in.astype(jnp.bfloat16), "dp", scatter_dimension=0, tiled=True
        ).astype(jnp.float32),
        lax.psum_scatter(
            grad_w_back.astype(jnp.bfloat16), "dp", scatter_dimension=0, tiled=True
        ).astype(jnp.float32),
    )
    qk_gains_grad = lax.psum(qk_partial, ("dp", "hg", "hid"))
    return (
        output,
        token_grad,
        norm_gain_grad,
        w_qkv_grad,
        qk_gains_grad,
        w_out_t_grad,
        w_in_grad,
        w_back_grad,
    )


def solution(mesh):
    return jax.shard_map(
        shards,
        mesh=mesh,
        in_specs=(
            P(("dp", "hid"), None),
            P(("dp", "hid")),
            P(),
            P(None, "hg"),
            P(),
            P(None, "hg"),
            P(None, ("hg", "hid")),
            P(None, ("hg", "hid")),
            P(("dp", "hid"), "hg"),
        ),
        out_specs=(
            P(("dp", "hid"), "hg"),
            P(("dp", "hid"), None),
            P(("dp", "hid")),
            P(("dp", "hid"), "hg"),
            P(),
            P(("dp", "hid"), "hg"),
            P("dp", ("hg", "hid")),
            P("dp", ("hg", "hid")),
        ),
        check_vma=False,
    )
```

profile of v0, /device:TPU:0, one launch (start us, length us, event | category | flops | bytes accessed | tf_op | source)
XLA Modules:
  0.0 659.8 jit_solution(1568707283787377378)
XLA Ops:
  8.0 34.2 %all-gather.6.cloned.1.call-done = bf16[1176,768]{1,0:T(8,128)(2,1)} async-done(((bf16[1176,384]{1,0:T(8,128)(2,1)}), bf16[1176,768]{1,0:T(8,128)(2,1)}) %all-gather.6.cloned.1.call-update) | async-done | bytes 1806352 | tf_op jit(solution)/shard_map/all_gather | solution.py:114
  48.1 4.0 fusion.76
  57.8 3.8 fusion.66
  61.7 3.0 copy.43
  70.8 8.3 %fusion.77 = f32[2352,768]{1,0:T(8,128)} fusion(bf16[2352,768]{1,0:T(8,128)(2,1)} %all-gather.8.cloned.1.call-done, bf16[768,768]{1,0:T(8,128)(2,1)} %param.20), kind=kOutput, calls=%fused_computation.143 | convolution fusion | flops 2774532096 | bytes 12017664 | tf_op jit(solution)/shard_map/dot_general | solution.py:137
  79.1 11.3 %fusion.54 = (bf16[2352,768]{1,0:T(8,128)(2,1)S(1)}, f32[2352,768]{1,0:T(8,128)}) fusion(f32[2352,768]{1,0:T(8,128)} %fusion.77, bf16[2352,768]{1,0:T(8,128)(2,1)} %all-gather.4.cloned.1.call-done, bf16[768,768]{1,0:T(8,128)(2,1)} %param.19), kind=kOutput, calls=%fused_computation.61 | convolution fusion | flops 2810658816 | bytes 22855680 | tf_op jit(solution)/shard_map/dot_general | solution.py:105
  92.3 4.6 convolution_convert_fusion
  98.1 33.9 %while.30 = (s32[]{:T(128)}, bf16[6,1,1176,64]{2,3,1,0:T(8,128)(2,1)S(1)}, f32[6,1,1176]{2,1,0:T(1,128)S(1)}, bf16[6,1,1176,64]{3,2,1,0:T(8,128)(2,1)}, bf16[6,1...) while((s32[]{:T(128)}, ...), condition=%wide.region_9.10_spmd.clone.clone, body=%wide.region_6.9_spmd.clone.sunk.clone | while | flops 366487456 | bytes 18392728 | solution.py:75
  132.5 3.5 convolution_convert_fusion.2
  138.3 9.6 %convolution_convert_fusion.1 = bf16[2352,768]{1,0:T(8,128)(2,1)} fusion(bf16[768,768]{1,0:T(8,128)(2,1)} %param.20, f32[2352,768]{1,0:T(8,128)} %get-tuple-element.296), kind=kOutput, calls=%fused_computation.64 | convolution fusion | flops 2792595456 | bytes 12017664 | tf_op jit(solution)/shard_map/dot_general | solution.py:24
  149.1 78.9 %while.31 = (s32[]{:T(128)}, f32[6,1,1176,64]{2,3,1,0:T(8,128)}, f32[6,1,1176,64]{2,3,1,0:T(8,128)}, bf16[6,1,1176,64]{2,3,1,0:T(8,128)(2,1)S(1)}, bf16[6,1,1176...) while((s32[]{:T(128)}, f32[6,1,1176,64]{2,3,1,0:T(8,128)}, ...), condition=%wide.region_14.15_spmd.clone.clone, body=%wide.region_12.14_spmd.clone.sunk.clone | while | flops 898933184 | bytes 44843632 | solution.py:75
  149.3 2.9 fusion.147
  162.5 2.9 fusion.147
  228.1 9.3 %fusion.64 = bf16[768,768]{0,1:T(8,128)(2,1)} fusion(bf16[2352,768]{1,0:T(8,128)(2,1)} %all-gather.8.cloned.1.call-done, f32[2352,768]{1,0:T(8,128)} %get-tuple-element.296), kind=kOutput, calls=%fused_computation.109 | convolution fusion | flops 2791378944 | bytes 12017664 | tf_op jit(solution)/shard_map/dot_general | solution.py:30
  240.1 5.5 fusion.56
  247.6 4.4 convolution_convert_fusion.4
  253.6 4.1 fusion.68
  260.1 7.0 %convolution_add_fusion.1 = f32[1176,768]{1,0:T(8,128)} fusion(bf16[1176,1152]{0,1:T(8,128)(2,1)} %bitcast.277, bf16[768,1152]{1,0:T(8,128)(2,1)S(1)} %copy-done, bf16[1176,768]{1,0:T(8,128)(2,1)} %reduce-scatter.16.cloned.1.call-done), kind=kOutput, calls=%fused_computation.66 | convolution fusion | flops 2082705408 | bytes 9897984 | tf_op jit(solution)/shard_map/dot_general | solution.py:24
  268.3 4.5 convolution_add_fusion
  272.9 3.5 convolution_bitcast_fusion.2
  279.4 6.9 %fusion.78 = f32[768,1152]{1,0:T(8,128)} fusion(bf16[1176,768]{1,0:T(8,128)(2,1)} %multiply_convert_fusion.2, bf16[1176,1152]{0,1:T(8,128)(2,1)} %bitcast.278), kind=kOutput, calls=%fused_computation.144 | convolution fusion | flops 2080899072 | bytes 8054784 | tf_op jit(solution)/shard_map/dot_general | solution.py:30
  286.4 3.7 convert_element_type.106
  291.3 40.1 %psum.15 = f32[2,64]{1,0:T(2,128)} all-reduce(f32[2,64]{1,0:T(2,128)S(1)} %pad_maximum_fusion.1), channel_id=1, replica_groups=mesh['dp'=8,'hg'=2,'hid'=2] {'dp','hg','hid'}, use_global_device_ids=true, to_apply=%region_28.29 | all-reduce | flops 128 | bytes 1024 | tf_op jit(solution)/shard_map/psum | solution.py:162
  333.4 37.8 %reduce-scatter.20.cloned.1.call-done = bf16[96,768]{1,0:T(8,128)(2,1)} async-done(((bf16[768,768]{1,0:T(8,128)(2,1)}), bf16[96,768]{1,0:T(8,128)(2,1)}) %reduce-scatter.20.cloned.1.call-update) | async-done | bytes 147472 | tf_op jit(solution)/shard_map/reduce_scatter | solution.py:155
  372.8 95.6 %all-reduce.3.cloned.1.call-done = f32[1176,768]{1,0:T(8,128)} async-done(((f32[1176,768]{1,0:T(8,128)}), f32[1176,768]{1,0:T(8,128)}) %all-reduce.3.cloned.1.call-update) | async-done | bytes 3612688 | tf_op jit(solution)/shard_map/psum | solution.py:144
  468.4 4.1 multiply_reduce_fusion.1
  472.5 33.2 %all-reduce = f32[768]{0:T(1024)S(1)} all-reduce(f32[768]{0:T(1024)S(1)} %get-tuple-element.240), channel_id=5, replica_groups=mesh['dp'=8,'hg'=2,'hid'=2] {'dp','hid'}, use_global_device_ids=true, to_apply=%region_24.25.clone | all-reduce | flops 768 | bytes 6144
  506.2 4.7 add_convert_fusion
  511.0 8.4 %reduce-scatter.14.cloned.1.call-done = f32[1176,384]{1,0:T(8,128)} async-done(((f32[1176,768]{1,0:T(8,128)}), f32[1176,384]{1,0:T(8,128)}) %reduce-scatter.14.cloned.1.call-update) | async-done | bytes 1806352 | tf_op jit(solution)/shard_map/reduce_scatter | solution.py:110
  519.3 3.1 add_convert_fusion.1
  522.5 58.9 %reduce-scatter.22.cloned.1.call-done = f32[48,384]{1,0:T(8,128)} async-done(((f32[768,384]{1,0:T(8,128)}), f32[48,384]{1,0:T(8,128)}) %reduce-scatter.22.cloned.1.call-update) | async-done | bytes 73744
  581.4 71.6 %reduce-scatter.18.cloned.1.call-done = f32[48,1152]{1,0:T(8,128)} async-done(((f32[768,1152]{1,0:T(8,128)}), f32[48,1152]{1,0:T(8,128)}) %reduce-scatter.18.cloned.1.call-update) | async-done | bytes 221200 | tf_op jit(solution)/shard_map/reduce_scatter | solution.py:150
  (203 shorter events, 148.3 us)
Async XLA Ops:
  7.2 40.9 %copy-start = (bf16[768,1152]{1,0:T(8,128)(2,1)S(1)}, bf16[768,1152]{1,0:T(8,128)(2,1)}, u32[]{:S(2)}) copy-start(bf16[768,1152]{1,0:T(8,128)(2,1)} %param.16) | copy-start | bytes 5308420
  7.2 35.0 %all-gather.6.cloned.1.call-start = ((), (), s32[]{:S(2)}) async-start(), calls=%async_computation.10 | async-start | bytes 2709504 | tf_op jit(solution)/shard_map/all_gather | solution.py:114
  7.9 62.8 %all-gather.8.cloned.1.call-start = ((), (), s32[]{:S(2)}) async-start(), calls=%async_computation.11 | async-start | bytes 5419008 | tf_op jit(solution)/shard_map/all_gather | solution.py:136
  42.2 36.9 %all-gather.4.cloned.1.call-start = ((), (), s32[]{:S(2)}) async-start(), calls=%async_computation.7 | async-start | bytes 5419008 | tf_op jit(solution)/shard_map/all_gather | solution.py:104
  48.0 212.0 %reduce-scatter.16.cloned.1.call-start = ((), (), s32[]{:S(2)}) async-start(), calls=%async_computation.12 | async-start | bytes 5419008 | tf_op jit(solution)/shard_map/reduce_scatter | solution.py:141
  52.2 2.9 copy-start.27
  55.0 6.6 %copy-start.9 = (f32[1176,6]{0,1:T(8,128)}, f32[1176,6]{0,1:T(8,128)S(1)}, u32[]{:S(2)}) copy-start(f32[1176,6]{0,1:T(8,128)S(1)} %broadcast_multiply_fusion.4) | copy-start | bytes 84676
  55.1 6.6 copy-start.24
  55.1 6.6 copy-start.11
  57.8 3.8 copy-start.13
  57.8 3.8 copy-start.15
  70.0 9.0 %copy-start.3 = (bf16[6,1,1176,64]{2,3,1,0:T(8,128)(2,1)}, bf16[6,1,1176,64]{2,3,1,0:T(8,128)(2,1)S(1)}, u32[]{:S(2)}) copy-start(bf16[6,1,1176,64]{2,3,1,0:T(8,128)(2,1)S(1)} %fusion.75) | copy-start | bytes 2709508
  79.1 13.2 %copy-start.29 = (bf16[768,768]{1,0:T(8,128)(2,1)S(1)}, bf16[768,768]{1,0:T(8,128)(2,1)}, u32[]{:S(2)}) copy-start(bf16[768,768]{1,0:T(8,128)(2,1)} %param.19) | copy-start | bytes 3538948
  96.9 170.3 %reduce-scatter.12.cloned.1.call-start = ((), (), s32[]{:S(2)}) async-start(), calls=%async_computation.8 | async-start | bytes 5419008 | tf_op jit(solution)/shard_map/reduce_scatter | solution.py:107
  98.1 34.5 %copy-start.17 = (bf16[768,384]{1,0:T(8,128)(2,1)S(1)}, bf16[768,384]{1,0:T(8,128)(2,1)}, u32[]{:S(2)}) copy-start(bf16[768,384]{1,0:T(8,128)(2,1)} %param.18) | copy-start | bytes 1769476
  131.9 4.1 copy-start.5
  148.0 183.5 %reduce-scatter.24.cloned.1.call-start = ((), (), s32[]{:S(2)}) async-start(), calls=%async_computation.17 | async-start | bytes 1327104
  237.3 2.8 copy-start.14
  237.3 2.8 copy-start.16
  237.4 2.8 copy-start.25
  239.8 131.3 %reduce-scatter.20.cloned.1.call-start = ((), (), s32[]{:S(2)}) async-start(), calls=%async_computation.15 | async-start | bytes 1327104 | tf_op jit(solution)/shard_map/reduce_scatter | solution.py:155
  240.1 7.4 %copy-start.28 = (bf16[2352,768]{1,0:T(8,128)(2,1)S(1)}, bf16[2352,768]{1,0:T(8,128)(2,1)}, u32[]{:S(2)}) copy-start(bf16[2352,768]{1,0:T(8,128)(2,1)} %all-gather.4.cloned.1.call-done) | copy-start | bytes 10838020
  240.1 7.4 %copy-start.32 = (bf16[2352,768]{1,0:T(8,128)(2,1)S(1)}, bf16[2352,768]{1,0:T(8,128)(2,1)}, u32[]{:S(2)}) copy-start(bf16[2352,768]{1,0:T(8,128)(2,1)} %copy-done.31) | copy-start | bytes 10838020
  252.0 216.4 %all-reduce.3.cloned.1.call-start = ((), (), s32[]{:S(2)}) async-start(), calls=%async_computation.13 | async-start | bytes 7225344 | tf_op jit(solution)/shard_map/psum | solution.py:144
  267.1 252.2 %reduce-scatter.14.cloned.1.call-start = ((), (), s32[]{:S(2)}) async-start(), calls=%async_computation.9 | async-start | bytes 5419008 | tf_op jit(solution)/shard_map/reduce_scatter | solution.py:110
  272.8 308.6 %reduce-scatter.22.cloned.1.call-start = ((), (), s32[]{:S(2)}) async-start(), calls=%async_computation.16 | async-start | bytes 1253376
  279.1 374.0 %reduce-scatter.18.cloned.1.call-start = ((), (), s32[]{:S(2)}) async-start(), calls=%async_computation.14 | async-start | bytes 3760128 | tf_op jit(solution)/shard_map/reduce_scatter | solution.py:150
  286.3 3.7 copy-start.30
  286.4 5.0 copy-start.26
  286.4 182.0 %copy-start.19 = (f32[1176]{0:T(1024)S(1)}, f32[1176]{0:T(1024)}, u32[]{:S(2)}) copy-start(f32[1176]{0:T(1024)} %copy-done.18) | copy-start | bytes 14116
  286.4 182.0 %copy-start.21 = (f32[1176]{0:T(1024)S(1)}, f32[1176]{0:T(1024)}, u32[]{:S(2)}) copy-start(f32[1176]{0:T(1024)} %copy-done.20) | copy-start | bytes 14116
  286.4 182.0 %copy-start.23 = (f32[768]{0:T(1024)S(1)}, f32[768]{0:T(1024)}, u32[]{:S(2)}) copy-start(f32[768]{0:T(1024)} %copy-done.22) | copy-start | bytes 9220
  (12 other events, 21.8 us)
Sparse Core Ops, SparseCore 0:
  9.6 32.5 all-gather.5
  43.7 12.8 all-gather.7
  58.7 13.9 all-gather.3
  97.0 11.8 reduce-scatter.15
  148.1 12.0 reduce-scatter.11
  239.9 64.7 reduce-scatter.23
  308.1 63.0 reduce-scatter.19
  373.5 94.8 all-reduce.2
  470.7 48.6 reduce-scatter.13
  523.4 57.9 reduce-scatter.21
  585.9 67.1 reduce-scatter.17
where the time goes:
time: 666 us; the launch traced here: 660 us
  waiting for transfers between devices  307 us (46%)
  matrix products  177 us (27%)
  blocking collectives  73.2 us (11%)
  other arithmetic  52.7 us (8%)
  local copies, waits for them, and re-layouts  31.1 us (5%)
  between operations  15.9 us (2%)
    psum x1, waiting for transfers between devices, shards(): grad_normed = lax.psum(grad_normed_att + grad_normed_mlp, 'hg')  95.6 us
    reduce_scatter x1, waiting for transfers between devices, shards(): lax.psum_scatter(grad_w_qkv, ('dp', 'hid'), scatter_dimension=0, tiled=True)  71.6 us
    unnamed x13, waiting for transfers between devices  59.8 us
    psum x1, blocking collectives, shards(): qk_gains_grad = lax.psum(qk_partial, ('dp', 'hg', 'hid'))  40.1 us
    reduce_scatter x1, waiting for transfers between devices, shards(): lax.psum_scatter(grad_w_in.astype(jnp.bfloat16), 'dp', scatter_dimension=...  37.8 us
    all_gather x1, waiting for transfers between devices, shards(): grad_out = lax.all_gather(cotangent, 'hg', axis=1, tiled=True)  34.2 us
    unnamed x1, blocking collectives  33.2 us
    dot_general x12, matrix products, masked_scores(): jnp.einsum('gqe,gke->gqk', queries, keys_in, preferred_element_type=jnp.f...  32.3 us
  transfers between devices with their start and end apart: 11, of which 6 were waited for; matrix products, arithmetic and copies ran while one was open for 36% of the time, Pallas kernels for 0%

commit v1 on v0

--- a/solution.py
+++ b/solution.py
@@ -76,14 +76,71 @@
     return tuple((member.reshape((heads_here, tok_rows) + member.shape[3:]) for member in results))
 
 
+def swap(value, axis, bit):
+    size = lax.axis_size(axis)
+    return lax.ppermute(value, axis, [(place, place ^ bit) for place in range(size)])
+
+
+def bits_of(axis):
+    size = lax.axis_size(axis)
+    return [1 << place for place in range(size.bit_length() - 1)]
+
+
+def gather_columns(block, axis):
+    for bit in bits_of(axis):
+        block = jnp.concatenate([block, swap(block, axis, bit)], axis=1)
+    return block
+
+
+def scatter_columns(grad, axis):
+    for bit in reversed(bits_of(axis)):
+        half = grad.shape[1] // 2
+        sent = swap(grad[:, half:].astype(jnp.bfloat16), axis, bit)
+        grad = grad[:, :half] + sent.astype(jnp.float32)
+    return grad
+
+
+def scatter_rows(grad, axes):
+    levels = []
+    for axis in axes:
+        levels += [(axis, bit) for bit in reversed(bits_of(axis))]
+    rows, columns = grad.shape
+    blocks = rows >> len(levels)
+    shaped = grad.reshape((2,) * len(levels) + (blocks, columns))
+    for axis, bit in reversed(levels):
+        place = len(shaped.shape) - 3
+        mine = (lax.axis_index(axis) & bit) > 0
+        low, high = (lax.index_in_dim(shaped, side, place, keepdims=False) for side in (0, 1))
+        sent = jnp.where(mine, low, high).astype(jnp.bfloat16)
+        shaped = jnp.where(mine, high, low) + swap(sent, axis, bit).astype(jnp.float32)
+    return shaped
+
+
+def sum_everywhere(value, axes):
+    for axis in axes:
+        for bit in bits_of(axis):
+            value = value + swap(value, axis, bit)
+    return value
+
+
+def both_halves(mine, axis):
+    other = swap(mine, axis, 1)
+    first = lax.axis_index(axis) == 0
+    return jnp.concatenate(
+        [jnp.where(first, mine, other), jnp.where(first, other, mine)], axis=1
+    )
+
+
 def shards(tokens, big_images, norm_gain, w_qkv, qk_gains, w_out_t, w_in, w_back, cotangent):
-    tok_rows = tokens.shape[0]
-    width = tokens.shape[1]
+    tok_rows, width = tokens.shape
     head_size = qk_gains.shape[1]
     heads_here = w_qkv.shape[1] // (3 * head_size)
     half_width = heads_here * head_size
     big_flag = big_images[0]
     head_scale = head_size ** (-0.5)
+    grad_out = both_halves(cotangent, "hg")
+    w_in = gather_columns(w_in, "hid")
+    w_back = gather_columns(w_back, "hid")
     inputs = tokens.astype(jnp.float32)
     normed, inverse = normalize(inputs)
     gain_vec = norm_gain.astype(jnp.float32)
@@ -100,19 +157,23 @@
     values_in = joined[:, :, 2].astype(jnp.bfloat16).transpose(1, 0, 2)
     attended, log_total = attention_pass(head_forward, (queries, keys_in, values_in), big_flag)
     attended_low = attended.astype(jnp.bfloat16).transpose(1, 0, 2).reshape(tok_rows, half_width)
-    attn_part = times_t(attended_low, w_out_t)
-    normed_all = lax.all_gather(normed_low, "hid", axis=0, tiled=True)
-    hidden_pre = jnp.dot(normed_all, w_in, preferred_element_type=jnp.float32)
+    hidden_pre = jnp.dot(normed_low, w_in, preferred_element_type=jnp.float32)
     hidden_act = jax.nn.gelu(hidden_pre).astype(jnp.bfloat16)
-    mlp_part = lax.psum_scatter(
-        times_t(hidden_act, w_back).astype(jnp.bfloat16), "hid", scatter_dimension=0, tiled=True
-    ).astype(jnp.float32)
-    mixed = lax.psum_scatter(attn_part + mlp_part, "hg", scatter_dimension=1, tiled=True)
+    mixed = times_t(attended_low, w_out_t) + times_t(hidden_act, w_back)
     out_cols = width // lax.axis_size("hg")
-    input_cols = lax.dynamic_slice_in_dim(inputs, lax.axis_index("hg") * out_cols, out_cols, 1)
-    output = (input_cols + mixed).astype(jnp.bfloat16)
-    grad_out = lax.all_gather(cotangent, "hg", axis=1, tiled=True)
-    grad_w_out = rows_t(grad_out, attended_low)
+    place = lax.axis_index("hg") * out_cols
+    sent = lax.dynamic_slice_in_dim(mixed, out_cols - place, out_cols, 1).astype(jnp.bfloat16)
+    kept = lax.dynamic_slice_in_dim(mixed + inputs, place, out_cols, 1)
+    output = (kept + swap(sent, "hg", 1).astype(jnp.float32)).astype(jnp.bfloat16)
+
+    grad_act = jnp.dot(grad_out, w_back, preferred_element_type=jnp.float32)
+    grad_up = jax.vjp(jax.nn.gelu, hidden_pre)[1](grad_act)[0].astype(jnp.bfloat16)
+    grad_w_back = scatter_columns(rows_t(grad_out, hidden_act), "hid")
+    grad_w_in = scatter_columns(rows_t(normed_low, grad_up), "hid")
+    w_in_grad = scatter_rows(grad_w_in, ("dp",))
+    w_back_grad = scatter_rows(grad_w_back, ("dp",))
+    w_out_t_grad = scatter_rows(rows_t(grad_out, attended_low), ("dp", "hid"))
+
     grad_attended = jnp.dot(grad_out, w_out_t, preferred_element_type=jnp.float32)
     grad_att_low = (
         grad_attended.astype(jnp.bfloat16)
@@ -131,35 +192,22 @@
     grad_k_raw = normalize_back(grad_key * k_gain, k_hat, k_inverse)
     grad_joined = jnp.stack([grad_q_raw, grad_k_raw, grad_values.transpose(1, 0, 2)], axis=2)
     grad_joined = grad_joined.reshape(tok_rows, 3 * half_width).astype(jnp.bfloat16)
-    grad_w_qkv = rows_t(normed_low, grad_joined)
-    grad_normed_att = times_t(grad_joined, w_qkv)
-    grad_out_all = lax.all_gather(grad_out, "hid", axis=0, tiled=True)
-    grad_act = jnp.dot(grad_out_all, w_back, preferred_element_type=jnp.float32)
-    grad_up = jax.vjp(jax.nn.gelu, hidden_pre)[1](grad_act)[0].astype(jnp.bfloat16)
-    grad_w_back = rows_t(grad_out_all, hidden_act)
-    grad_w_in = rows_t(normed_all, grad_up)
-    grad_normed_mlp = lax.psum_scatter(
-        times_t(grad_up, w_in).astype(jnp.bfloat16), "hid", scatter_dimension=0, tiled=True
-    ).astype(jnp.float32)
-    grad_normed = lax.psum(grad_normed_att + grad_normed_mlp, "hg")
+    grad_normed = times_t(grad_joined, w_qkv) + times_t(grad_up, w_in)
+    normed_sent = grad_normed.astype(jnp.bfloat16)
+    w_qkv_grad = scatter_rows(rows_t(normed_low, grad_joined), ("dp", "hid"))
+    gain_partial = jnp.sum(grad_normed * normed, axis=0)
+    small = sum_everywhere(
+        jnp.concatenate([gain_partial, qk_partial.reshape(-1)]), ("hid", "hg", "dp")
+    )
+    shard_count = lax.axis_size("dp") * lax.axis_size("hid")
+    own = lax.axis_index("dp") * lax.axis_size("hid") + lax.axis_index("hid")
+    gain_rows = width // shard_count
+    norm_gain_grad = lax.dynamic_slice_in_dim(small, own * gain_rows, gain_rows, 0)
+    qk_gains_grad = small[width:].reshape(2, head_size)
+    grad_normed = normed_sent.astype(jnp.float32) + swap(normed_sent, "hg", 1).astype(jnp.float32)
     token_grad = (
         normalize_back(grad_normed * gain_vec, normed, inverse) + grad_out.astype(jnp.float32)
     ).astype(jnp.bfloat16)
-    gain_partial = jnp.sum(grad_normed * normed, axis=0)
-    w_qkv_grad, w_out_t_grad, norm_gain_grad = (
-        lax.psum_scatter(grad_w_qkv, ("dp", "hid"), scatter_dimension=0, tiled=True),
-        lax.psum_scatter(grad_w_out, ("dp", "hid"), scatter_dimension=0, tiled=True),
-        lax.psum_scatter(gain_partial, ("dp", "hid"), scatter_dimension=0, tiled=True),
-    )
-    w_in_grad, w_back_grad = (
-        lax.psum_scatter(
-            grad_w_in.astype(jnp.bfloat16), "dp", scatter_dimension=0, tiled=True
-        ).astype(jnp.float32),
-        lax.psum_scatter(
-            grad_w_back.astype(jnp.bfloat16), "dp", scatter_dimension=0, tiled=True
-        ).astype(jnp.float32),
-    )
-    qk_gains_grad = lax.psum(qk_partial, ("dp", "hg", "hid"))
     return (
         output,
         token_grad,

time: 666 us -> 338 us (0.51)
  waiting for transfers between devices: 307 us -> 56.9 us
  blocking collectives: 73.2 us -> 0 us
  matrix products: 177 us -> 149 us
  starting transfers between devices: 0.91 us -> 27.5 us
  between operations: 15.9 us -> 2.61 us
  other arithmetic: 52.7 us -> 61 us
    reduce_scatter x5 -> x0, waiting for transfers between devices: 118 us -> none  [the longest x1 71.6 us: shards(): lax.psum_scatter(grad_w_qkv, ('dp', 'hid'), scatter_dimension=0, tiled=True)]
    psum x1 -> x0, waiting for transfers between devices: 95.6 us -> none  [shards(): grad_normed = lax.psum(grad_normed_att + grad_normed_mlp, 'hg')]
    unnamed x13 -> x0, waiting for transfers between devices: 59.8 us -> none
    ppermute x0 -> x26, waiting for transfers between devices: none -> 56.9 us  [swap(): lax.ppermute(value, axis, [(place, place ^ bit) for place in range(size)])]
    psum x1 -> x0, blocking collectives: 40.1 us -> none  [shards(): qk_gains_grad = lax.psum(qk_partial, ('dp', 'hg', 'hid'))]
    all_gather x3 -> x0, waiting for transfers between devices: 34.2 us -> none  [the longest x1 34.2 us: shards(): grad_out = lax.all_gather(cotangent, 'hg', axis=1, tiled=True)]
    unnamed x1 -> x0, blocking collectives: 33.2 us -> none
    ppermute x0 -> x26, starting transfers between devices: none -> 27.5 us  [swap(): lax.ppermute(value, axis, [(place, place ^ bit) for place in range(size)])]
  transfers between devices with their start and end apart: 11 -> 26, of which waited for: 6 -> 10; matrix products, arithmetic and copies ran while one was open for 36% -> 72% of each run, Pallas kernels for 0% -> 0%
where the time goes in v1:
time: 338 us; the launch traced here: 333 us
  matrix products  149 us (44%)
  other arithmetic  61 us (18%)
  waiting for transfers between devices  56.9 us (17%)
  local copies, waits for them, and re-layouts  35.3 us (10%)
  starting transfers between devices  27.5 us (8%)
    ppermute x26, waiting for transfers between devices, swap(): lax.ppermute(value, axis, [(place, place ^ bit) for place in range(size)])  56.9 us
    dot_general x12, matrix products, masked_scores(): jnp.einsum('gqe,gke->gqk', queries, keys_in, preferred_element_type=jnp.f...  32.2 us
    ppermute x26, starting transfers between devices, swap(): lax.ppermute(value, axis, [(place, place ^ bit) for place in range(size)])  27.5 us
    dot_general x4, matrix products, times_t(): lax.dot_general(left, right, (((1,), (1,)), ((), ())), preferred_element_...  19.5 us
    unnamed x109, local copies, waits for them, and re-layouts  16.8 us
    dot_general x6, matrix products, head_back(): jnp.einsum('gqk,gqe->gke', grad_scores, queries, preferred_element_type=j...  16.4 us
    dot_general x6, matrix products, head_back(): jnp.einsum('gqk,gke->gqe', grad_scores, keys_in, preferred_element_type=j...  14.5 us
    dot_general x4, matrix products, rows_t(): lax.dot_general(left, right, (((0,), (0,)), ((), ())), preferred_element_...  13.6 us
  transfers between devices with their start and end apart: 26, of which 10 were waited for; matrix products, arithmetic and copies ran while one was open for 72% of the time, Pallas kernels for 0%

profile of v1, /device:TPU:0, one launch (start us, length us, event | category | flops | bytes accessed | tf_op | source)
XLA Modules:
  0.0 332.7 jit_solution(11380603064540914625)
XLA Ops:
  0.6 3.0 collective-permute-start.3
  7.7 2.9 fusion.105
  14.9 2.9 copy.61
  20.6 4.0 %fusion.70 = (bf16[6,1,1176,64]{2,3,0,1:T(8,128)(2,1)}, bf16[6,1,1176,64]{2,3,0,1:T(8,128)(2,1)}) fusion(f32[64]{0:T(128)S(1)} %get-tuple-element.257, f32[1176,6]{0,1:T(8,128)S(1)} %get-tuple-element.261, f32[1176,6]{0,1:T(8,128)S(1)} %broadcast_multiply_fusion.4, f32[1176,6,3,64]{0,3,2,1:T(8,128)} %bitcast.411, f32[64]{0:T(128)S(1)} %get-tuple-element.258, ...), kind=kLoop, calls=%fused_computation.122 | loop fusion | flops 4064256 | bytes 5532416 | tf_op jit(solution)/shard_map/reshape | solution.py:73
  30.0 33.3 %while.30 = (s32[]{:T(128)}, bf16[6,1,1176,64]{2,3,1,0:T(8,128)(2,1)S(1)}, f32[6,1,1176]{2,1,0:T(1,128)S(1)}, bf16[6,1,1176,64]{3,2,1,0:T(8,128)(2,1)}, bf16[6,1...) while((s32[]{:T(128)}, ...), condition=%wide.region_9.10_spmd.clone.clone, body=%wide.region_6.9_spmd.clone.sunk.clone | while | flops 366487456 | bytes 18392736 | solution.py:75
  63.3 3.9 %convert_element_type.237 = f32[1176,768]{1,0:T(8,128)} convert(bf16[1176,768]{1,0:T(8,128)(2,1)} %param.13) | non-fusion elementwise | flops 903168 | bytes 5419008 | tf_op jit(solution)/shard_map/convert_element_type | solution.py:144
  71.1 3.1 fusion.111
  81.3 82.2 %while.31 = (s32[]{:T(128)}, f32[6,1,1176,64]{2,3,1,0:T(8,128)}, f32[6,1,1176,64]{2,3,1,0:T(8,128)}, bf16[6,1,1176,64]{2,3,1,0:T(8,128)(2,1)S(1)}, bf16[6,1,1176...) while((s32[]{:T(128)}, f32[6,1,1176,64]{2,3,1,0:T(8,128)}, ...), condition=%wide.region_12.13_spmd.clone.clone, body=%wide.region_10.12_spmd.clone.sunk.clone | while | flops 898933184 | bytes 44843640 | solution.py:75
  109.1 2.9 fusion.178
  149.9 2.9 fusion.178
  163.6 5.0 %fusion.57 = (f32[64]{0:T(128)S(1)}, f32[1176,6]{0,1:T(8,128)S(1)}, f32[1176,6]{0,1:T(8,128)S(1)}, f32[64]{0:T(128)S(1)}, f32[1176,6]{0,1:T(8,128)S(1)}, /*index=5*/f32[1176,6]{0,1:T(8,128)S(1)}) fusion(f32[6,1,1176,64]{2,3,1,0:T(8,128)} %get-tuple-element.102, f32[1176,6]{0,1:T(8,128)S(1)} %copy-done.38, f32[1176,6]{0,1:T(8,128)S(1)} %copy-done.33, ...), kind=kLoop, calls=%fused_computation.87 | loop fusion | flops 7648576 | bytes 7452160 | tf_op jit(solution)/shard_map/reduce_sum | solution.py:189
  168.7 3.5 %fusion.60 = (bf16[1176,6,1,64]{0,3,1,2:T(8,128)(2,1)S(1)}, bf16[1176,6,1,64]{0,3,1,2:T(8,128)(2,1)S(1)}) fusion(f32[6,1,1176,64]{2,3,1,0:T(8,128)S(1)} %copy-done.19, f32[1176,6]{0,1:T(8,128)S(1)} %broadcast_multiply_fusion.2, f32[1176,6]{0,1:T(8,128)S(1)} %broadcast_multiply_fusion.3, f32[64]{0:T(128)S(1)} %broadcast_multiply_fusion.9, ...), kind=kLoop, calls=%fused_computation.93 | loop fusion | flops 7225344 | bytes 9257984 | tf_op jit(solution)/shard_map/stack | solution.py:193
  174.1 4.1 %copy.82 = bf16[768,1176]{1,0:T(8,128)(2,1)} copy(bf16[768,1176]{0,1:T(8,128)(2,1)} %fusion.100) | data formatting | bytes 3612672 | tf_op jit(solution)/shard_map/dot_general | solution.py:30
  182.4 4.5 %fusion.112 = f32[1176,768]{1,0:T(8,128)} fusion(bf16[1176,1152]{0,1:T(8,128)(2,1)S(1)} %bitcast.420, bf16[768,1152]{1,0:T(8,128)(2,1)S(1)} %copy-done), kind=kOutput, calls=%fused_computation.213 | convolution fusion | flops 2080899072 | bytes 8091648 | tf_op jit(solution)/shard_map/dot_general | solution.py:24
  188.3 3.2 fusion.104
  191.6 3.5 %fusion.99 = f32[768,1536]{1,0:T(8,128)S(1)} fusion(bf16[1176,384]{1,0:T(8,128)(2,1)S(1)} %copy-done.14, bf16[1176,384]{1,0:T(8,128)(2,1)S(1)} %copy-done.12, f32[1176,1536]{1,0:T(8,128)S(1)} %fusion.104), kind=kOutput, calls=%fused_computation.200 | convolution fusion | flops 2794401792 | bytes 13750272 | tf_op jit(solution)/shard_map/dot_general | solution.py:30
  196.5 6.7 %fusion.54 = bf16[1176,1536]{1,0:T(8,128)(2,1)S(1)} fusion(f32[1176,1536]{1,0:T(8,128)S(1)} %fusion.104, bf16[768,1536]{1,0:T(8,128)(2,1)S(1)} %constant_dynamic-update-slice_fusion.2, bf16[1176,384]{1,0:T(8,128)(2,1)S(1)} %copy-done.14, bf16[1176,384]{1,0:T(8,128)(2,1)S(1)} %copy-done.12), kind=kOutput, calls=%fused_computation.61 | convolution fusion | flops 2814271488 | bytes 15003648 | tf_op jit(solution)/shard_map/dot_general | solution.py:169
  203.2 6.9 %convolution_add_fusion.1 = f32[1176,768]{1,0:T(8,128)S(1)} fusion(f32[1176,768]{1,0:T(8,128)S(1)} %copy-done.5, bf16[768,1536]{1,0:T(8,128)(2,1)S(1)} %constant_dynamic-update-slice_fusion.2, f32[1176,1536]{1,0:T(8,128)} %copy-done.51), kind=kOutput, calls=%fused_computation.65 | convolution fusion | flops 2791692288 | bytes 16809984 | tf_op jit(solution)/shard_map/dot_general | solution.py:24
  212.8 3.8 %collective-permute-done.15 = bf16[2,2,48,384]{3,2,1,0:T(8,128)(2,1)S(1)} collective-permute-done((bf16[2,2,48,384]{3,2,1,0:T(8,128)(2,1)S(1)}, bf16[2,2,48,384]{3,2,1,0:T(8,128)(2,1)S(1)}, u32[]{:S(2)}, u32[]{:S(2)}) %collective-permute-start.15) | collective-permute-done | bytes 147488 | tf_op jit(solution)/shard_map/ppermute | solution.py:81
  218.3 5.1 %fusion.110 = (bf16[1176,768]{1,0:T(8,128)(2,1)S(1)}, f32[1176,768]{1,0:T(8,128)S(1)}) fusion(f32[1176,768]{1,0:T(8,128)} %fusion.112, bf16[1176,1536]{1,0:T(8,128)(2,1)S(1)} %fusion.54, bf16[768,1536]{1,0:T(8,128)(2,1)S(1)} %constant_dynamic-update-slice_fusion), kind=kOutput, calls=%fused_computation.211 | convolution fusion | flops 2776338432 | bytes 15003648 | tf_op jit(solution)/shard_map/dot_general | solution.py:24
  226.0 3.5 %fusion.102 = f32[768,1536]{1,0:T(8,128)S(1)} fusion(bf16[1176,1536]{1,0:T(8,128)(2,1)S(1)} %fusion.54, bf16[1176,768]{1,0:T(8,128)(2,1)S(1)} %copy-done.3, f32[768]{0:T(1024)S(1)} %copy-done.47, f32[1176]{0:T(1024)S(1)} %copy-done.45, f32[1176]{0:T(1024)S(1)} %copy-done.43), kind=kOutput, calls=%fused_computation.203 | convolution fusion | flops 2779047936 | bytes 10150080 | tf_op jit(solution)/shard_map/dot_general | solution.py:30
  237.1 10.9 %collective-permute-done.23 = bf16[2,2,96,768]{3,2,0,1:T(8,128)(2,1)S(1)} collective-permute-done((bf16[2,2,96,768]{3,2,0,1:T(8,128)(2,1)S(1)}, bf16[2,2,96,768]{3,2,0,1:T(8,128)(2,1)S(1)}, u32[]{:S(2)}, u32[]{:S(2)}) %collective-permute-start.23) | collective-permute-done | bytes 589856 | tf_op jit(solution)/shard_map/ppermute | solution.py:81
  249.5 10.3 %collective-permute-done.19 = bf16[2,2,96,768]{3,2,0,1:T(8,128)(2,1)S(1)} collective-permute-done((bf16[2,2,96,768]{3,2,0,1:T(8,128)(2,1)S(1)}, bf16[2,2,96,768]{3,2,0,1:T(8,128)(2,1)S(1)}, u32[]{:S(2)}, u32[]{:S(2)}) %collective-permute-start.19) | collective-permute-done | bytes 589856 | tf_op jit(solution)/shard_map/ppermute | solution.py:81
  262.4 10.5 %collective-permute-done.4 = bf16[1176,768]{1,0:T(8,128)(2,1)S(1)} collective-permute-done((bf16[1176,768]{1,0:T(8,128)(2,1)S(1)}, bf16[1176,768]{1,0:T(8,128)(2,1)S(1)}, u32[]{:S(2)}, u32[]{:S(2)}) %collective-permute-start.4) | collective-permute-done | bytes 1806368 | tf_op jit(solution)/shard_map/ppermute | solution.py:81
  272.8 3.6 %fusion.55 = (f32[1176]{0:T(1024)S(1)}, f32[1176]{0:T(1024)S(1)}, f32[768]{0:T(1024)S(1)}, bf16[768,1176]{0,1:T(8,128)(2,1)}) fusion(bf16[1176,768]{1,0:T(8,128)(2,1)S(1)} %collective-permute-done.4, bf16[1176,768]{1,0:T(8,128)(2,1)S(1)} %get-tuple-element.259, f32[768]{0:T(1024)S(1)} %copy-done.47, f32[1176]{0:T(1024)S(1)} %copy-done.45, ...), kind=kLoop, calls=%fused_computation.74 | loop fusion | flops 12641232 | bytes 10862976 | tf_op jit(solution)/shard_map/reduce_sum | solution.py:20
  276.5 3.9 %copy.68 = bf16[768,1176]{1,0:T(8,128)(2,1)} copy(bf16[768,1176]{0,1:T(8,128)(2,1)} %get-tuple-element.254) | data formatting | bytes 3612672 | tf_op jit(solution)/shard_map/dot_general | solution.py:30
  280.5 5.3 %fusion.113 = f32[2,2,2,2,48,1152]{5,4,3,2,1,0:T(8,128)S(1)} fusion(bf16[2,2,2,2,48,1176]{5,4,3,2,1,0:T(8,128)(2,1)} %bitcast.423, bf16[1176,1152,1,1,1,1]{0,1,5,4,3,2:T(8,128)(2,1)} %bitcast.421), kind=kOutput, calls=%fused_computation.214 | convolution fusion | flops 2080899072 | bytes 8054784 | tf_op jit(solution)/shard_map/dot_general | solution.py:30
  290.0 3.1 collective-permute-done.7
  299.4 3.0 add_convert_fusion
  311.3 7.0 %collective-permute-done.11 = bf16[2,2,48,1152]{3,2,1,0:T(8,128)(2,1)S(1)} collective-permute-done((bf16[2,2,48,1152]{3,2,1,0:T(8,128)(2,1)S(1)}, bf16[2,2,48,1152]{3,2,1,0:T(8,128)(2,1)S(1)}, u32[]{:S(2)}, u32[]{:S(2)}) %collective-permute-start.11) | collective-permute-done | bytes 442400 | tf_op jit(solution)/shard_map/ppermute | solution.py:81
  320.1 4.4 %collective-permute-done.12 = bf16[2,48,1152]{2,1,0:T(8,128)(2,1)S(1)} collective-permute-done((bf16[2,48,1152]{2,1,0:T(8,128)(2,1)S(1)}, bf16[2,48,1152]{2,1,0:T(8,128)(2,1)S(1)}, u32[]{:S(2)}, u32[]{:S(2)}) %collective-permute-start.12) | collective-permute-done | bytes 221216 | tf_op jit(solution)/shard_map/ppermute | solution.py:81
  324.6 3.5 %collective-permute-start.13 = (bf16[48,1152]{1,0:T(8,128)(2,1)S(1)}, bf16[48,1152]{1,0:T(8,128)(2,1)S(1)}, u32[]{:S(2)}, u32[]{:S(2)}) collective-permute-start(bf16[48,1152]{1,0:T(8,128)(2,1)S(1)} %fusion.93), channel_id=1, source_target_pairs={{0,16},{4,20},{8,24},{12,28},{16,0},{20,4},{24,8},{28,12},{1,17},{... | collective-permute-start | bytes 331784 | tf_op jit(solution)/shard_map/ppermute | solution.py:81
  (302 shorter events, 188.2 us)
Async XLA Ops:
  0.6 73.5 %collective-permute-start.3 = (bf16[1176,384]{1,0:T(8,128)(2,1)}, bf16[1176,384]{1,0:T(8,128)(2,1)}, u32[]{:S(2)}, u32[]{:S(2)}) collective-permute-start(bf16[1176,384]{1,0:T(8,128)(2,1)} %param.21), channel_id=1, source_target_pairs={{0,2},{2,0},{1,3},{3,1},{4,6},{6,4},{5,7},{7,5},{8,10},{10,8},{9,1... | collective-permute-start | bytes 2709512 | tf_op jit(solution)/shard_map/ppermute | solution.py:81
  3.7 183.2 %collective-permute-start = (bf16[768,768]{1,0:T(8,128)(2,1)}, bf16[768,768]{1,0:T(8,128)(2,1)}, u32[]{:S(2)}, u32[]{:S(2)}) collective-permute-start(bf16[768,768]{1,0:T(8,128)(2,1)} %param.19), channel_id=1, source_target_pairs={{0,1},{1,0},{2,3},{3,2},{4,5},{5,4},{6,7},{7,6},{8,9},{9,8},{10,11... | collective-permute-start | bytes 3538952 | tf_op jit(solution)/shard_map/ppermute | solution.py:81
  3.7 191.4 %collective-permute-start.1 = (bf16[768,768]{1,0:T(8,128)(2,1)}, bf16[768,768]{1,0:T(8,128)(2,1)}, u32[]{:S(2)}, u32[]{:S(2)}) collective-permute-start(bf16[768,768]{1,0:T(8,128)(2,1)} %param.20), channel_id=1, source_target_pairs={{0,1},{1,0},{2,3},{3,2},{4,5},{5,4},{6,7},{7,6},{8,9},{9,8},{10,11... | collective-permute-start | bytes 3538952 | tf_op jit(solution)/shard_map/ppermute | solution.py:81
  81.3 82.2 %copy-start.31 = (f32[1176,6]{0,1:T(8,128)S(1)}, f32[1176,6]{0,1:T(8,128)}, u32[]{:S(2)}) copy-start(f32[1176,6]{0,1:T(8,128)} %copy-done.30) | copy-start | bytes 84676
  81.3 82.2 %copy-start.33 = (f32[1176,6]{0,1:T(8,128)S(1)}, f32[1176,6]{0,1:T(8,128)}, u32[]{:S(2)}) copy-start(f32[1176,6]{0,1:T(8,128)} %copy-done.32) | copy-start | bytes 84676
  81.3 82.2 %copy-start.36 = (f32[1176,6]{0,1:T(8,128)S(1)}, f32[1176,6]{0,1:T(8,128)}, u32[]{:S(2)}) copy-start(f32[1176,6]{0,1:T(8,128)} %copy-done.35) | copy-start | bytes 84676
  81.3 82.2 %copy-start.38 = (f32[1176,6]{0,1:T(8,128)S(1)}, f32[1176,6]{0,1:T(8,128)}, u32[]{:S(2)}) copy-start(f32[1176,6]{0,1:T(8,128)} %copy-done.37) | copy-start | bytes 84676
  81.3 82.2 %copy-start.49 = (f32[64]{0:T(128)S(1)}, f32[64]{0:T(128)}, u32[]{:S(2)}) copy-start(f32[64]{0:T(128)} %copy-done.48) | copy-start | bytes 772
  182.2 27.9 %collective-permute-start.14 = (bf16[2,2,2,48,384]{4,3,2,1,0:T(8,128)(2,1)S(1)}, bf16[2,2,2,48,384]{4,3,2,1,0:T(8,128)(2,1)S(1)}, u32[]{:S(2)}, u32[]{:S(2)}) collective-permute-start(bf16[2,2,2,48,384]{4,3,2,1,0:T(8,128)(2,1)S(1)} %fusion.82), channel_id=1, source_target_pairs={{0,1},{1,0},{2,3},{3,2},{4,5},{5,4},{6,7},{7,6},{8,9},{9,8},{10,11... | collective-permute-start | bytes 884744 | tf_op jit(solution)/shard_map/ppermute | solution.py:81
  210.2 6.3 %collective-permute-start.15 = (bf16[2,2,48,384]{3,2,1,0:T(8,128)(2,1)S(1)}, bf16[2,2,48,384]{3,2,1,0:T(8,128)(2,1)S(1)}, u32[]{:S(2)}, u32[]{:S(2)}) collective-permute-start(bf16[2,2,48,384]{3,2,1,0:T(8,128)(2,1)S(1)} %fusion.88), channel_id=1, source_target_pairs={{0,4},{4,0},{8,12},{12,8},{16,20},{20,16},{24,28},{28,24},{1,5},{5... | collective-permute-start | bytes 442376 | tf_op jit(solution)/shard_map/ppermute | solution.py:81
  211.9 23.0 %collective-permute-start.2 = (bf16[1176,384]{1,0:T(8,128)(2,1)S(1)}, bf16[1176,384]{1,0:T(8,128)(2,1)S(1)}, u32[]{:S(2)}, u32[]{:S(2)}) collective-permute-start(bf16[1176,384]{1,0:T(8,128)(2,1)S(1)} %dynamic-slice_convert_fusion), channel_id=1, source_target_pairs={{0,2},{2,0},{1,3},{3,1},{4,6},{6,4},{5,7},{7,5},{8,10},{10,8},{9,1... | collective-permute-start | bytes 2709512 | tf_op jit(solution)/shard_map/ppermute | solution.py:81
  212.7 18.4 %collective-permute-start.22 = (bf16[768,768]{1,0:T(8,128)(2,1)S(1)}, bf16[768,768]{1,0:T(8,128)(2,1)S(1)}, u32[]{:S(2)}, u32[]{:S(2)}) collective-permute-start(bf16[768,768]{1,0:T(8,128)(2,1)S(1)} %slice.330), channel_id=1, source_target_pairs={{0,1},{1,0},{2,3},{3,2},{4,5},{5,4},{6,7},{7,6},{8,9},{9,8},{10,11... | collective-permute-start | bytes 3538952 | tf_op jit(solution)/shard_map/ppermute | solution.py:81
  216.6 6.7 %collective-permute-start.16 = (bf16[2,48,384]{2,1,0:T(8,128)(2,1)S(1)}, bf16[2,48,384]{2,1,0:T(8,128)(2,1)S(1)}, u32[]{:S(2)}, u32[]{:S(2)}) collective-permute-start(bf16[2,48,384]{2,1,0:T(8,128)(2,1)S(1)} %fusion.94), channel_id=1, source_target_pairs={{0,8},{4,12},{8,0},{12,4},{16,24},{20,28},{24,16},{28,20},{1,9},{5... | collective-permute-start | bytes 221192 | tf_op jit(solution)/shard_map/ppermute | solution.py:81
  223.3 49.5 %copy-start.23 = (bf16[1176,768]{1,0:T(8,128)(2,1)}, bf16[1176,768]{1,0:T(8,128)(2,1)S(1)}, u32[]{:S(2)}) copy-start(bf16[1176,768]{1,0:T(8,128)(2,1)S(1)} %get-tuple-element.259) | copy-start | bytes 5419012
  223.4 7.0 %collective-permute-start.17 = (bf16[48,384]{1,0:T(8,128)(2,1)S(1)}, bf16[48,384]{1,0:T(8,128)(2,1)S(1)}, u32[]{:S(2)}, u32[]{:S(2)}) collective-permute-start(bf16[48,384]{1,0:T(8,128)(2,1)S(1)} %fusion.95), channel_id=1, source_target_pairs={{0,16},{4,20},{8,24},{12,28},{16,0},{20,4},{24,8},{28,12},{1,17},{... | collective-permute-start | bytes 110600 | tf_op jit(solution)/shard_map/ppermute | solution.py:81
  229.8 3.6 %collective-permute-start.18 = (bf16[768,768]{1,0:T(8,128)(2,1)S(1)}, bf16[768,768]{1,0:T(8,128)(2,1)S(1)}, u32[]{:S(2)}, u32[]{:S(2)}) collective-permute-start(bf16[768,768]{1,0:T(8,128)(2,1)S(1)} %slice.331), channel_id=1, source_target_pairs={{0,1},{1,0},{2,3},{3,2},{4,5},{5,4},{6,7},{7,6},{8,9},{9,8},{10,11... | collective-permute-start | bytes 3538952 | tf_op jit(solution)/shard_map/ppermute | solution.py:81
  229.8 43.0 %collective-permute-start.4 = (bf16[1176,768]{1,0:T(8,128)(2,1)S(1)}, bf16[1176,768]{1,0:T(8,128)(2,1)S(1)}, u32[]{:S(2)}, u32[]{:S(2)}) collective-permute-start(bf16[1176,768]{1,0:T(8,128)(2,1)S(1)} %get-tuple-element.259), channel_id=1, source_target_pairs={{0,2},{2,0},{1,3},{3,1},{4,6},{6,4},{5,7},{7,5},{8,10},{10,8},{9,1... | collective-permute-start | bytes 5419016 | tf_op jit(solution)/shard_map/ppermute | solution.py:81
  231.8 16.2 %collective-permute-start.23 = (bf16[2,2,96,768]{3,2,0,1:T(8,128)(2,1)S(1)}, bf16[2,2,96,768]{3,2,0,1:T(8,128)(2,1)S(1)}, u32[]{:S(2)}, u32[]{:S(2)}) collective-permute-start(bf16[2,2,96,768]{3,2,0,1:T(8,128)(2,1)S(1)} %fusion.76), channel_id=1, source_target_pairs={{0,4},{4,0},{8,12},{12,8},{16,20},{20,16},{24,28},{28,24},{1,5},{5... | collective-permute-start | bytes 1769480 | tf_op jit(solution)/shard_map/ppermute | solution.py:81
  234.0 25.8 %collective-permute-start.19 = (bf16[2,2,96,768]{3,2,0,1:T(8,128)(2,1)S(1)}, bf16[2,2,96,768]{3,2,0,1:T(8,128)(2,1)S(1)}, u32[]{:S(2)}, u32[]{:S(2)}) collective-permute-start(bf16[2,2,96,768]{3,2,0,1:T(8,128)(2,1)S(1)} %fusion.75), channel_id=1, source_target_pairs={{0,4},{4,0},{8,12},{12,8},{16,20},{20,16},{24,28},{28,24},{1,5},{5... | collective-permute-start | bytes 1769480 | tf_op jit(solution)/shard_map/ppermute | solution.py:81
  249.1 54.5 %collective-permute-start.24 = (bf16[2,96,768]{2,1,0:T(8,128)(2,1)}, bf16[2,96,768]{2,1,0:T(8,128)(2,1)S(1)}, u32[]{:S(2)}, u32[]{:S(2)}) collective-permute-start(bf16[2,96,768]{2,1,0:T(8,128)(2,1)} %fusion.84), channel_id=1, source_target_pairs={{0,8},{4,12},{8,0},{12,4},{16,24},{20,28},{24,16},{28,20},{1,9},{5... | collective-permute-start | bytes 884744 | tf_op jit(solution)/shard_map/ppermute | solution.py:81
  261.9 47.8 %collective-permute-start.20 = (bf16[2,96,768]{2,1,0:T(8,128)(2,1)}, bf16[2,96,768]{2,1,0:T(8,128)(2,1)S(1)}, u32[]{:S(2)}, u32[]{:S(2)}) collective-permute-start(bf16[2,96,768]{2,1,0:T(8,128)(2,1)} %fusion.83), channel_id=1, source_target_pairs={{0,8},{4,12},{8,0},{12,4},{16,24},{20,28},{24,16},{28,20},{1,9},{5... | collective-permute-start | bytes 884744 | tf_op jit(solution)/shard_map/ppermute | solution.py:81
  276.5 9.4 %collective-permute-start.5 = (f32[896]{0:T(1024)S(1)}, f32[896]{0:T(1024)S(1)}, u32[]{:S(2)}, u32[]{:S(2)}) collective-permute-start(f32[896]{0:T(1024)S(1)} %pad_maximum_fusion.1), channel_id=1, source_target_pairs={{0,1},{1,0},{2,3},{3,2},{4,5},{5,4},{6,7},{7,6},{8,9},{9,8},{10,11... | collective-permute-start | bytes 10760 | tf_op jit(solution)/shard_map/ppermute | solution.py:81
  285.9 3.7 %collective-permute-start.6 = (f32[896]{0:T(1024)S(1)}, f32[896]{0:T(1024)S(1)}, u32[]{:S(2)}, u32[]{:S(2)}) collective-permute-start(f32[896]{0:T(1024)S(1)} %fusion.133), channel_id=1, source_target_pairs={{0,2},{2,0},{1,3},{3,1},{4,6},{6,4},{5,7},{7,5},{8,10},{10,8},{9,1... | collective-permute-start | bytes 10760 | tf_op jit(solution)/shard_map/ppermute | solution.py:81
  289.5 3.6 %collective-permute-start.7 = (f32[896]{0:T(1024)S(1)}, f32[896]{0:T(1024)S(1)}, u32[]{:S(2)}, u32[]{:S(2)}) collective-permute-start(f32[896]{0:T(1024)S(1)} %add.175), channel_id=1, source_target_pairs={{0,4},{4,0},{8,12},{12,8},{16,20},{20,16},{24,28},{28,24},{1,5},{5... | collective-permute-start | bytes 10760 | tf_op jit(solution)/shard_map/ppermute | solution.py:81
  293.1 3.6 %collective-permute-start.8 = (f32[896]{0:T(1024)S(1)}, f32[896]{0:T(1024)S(1)}, u32[]{:S(2)}, u32[]{:S(2)}) collective-permute-start(f32[896]{0:T(1024)S(1)} %add.176), channel_id=1, source_target_pairs={{0,8},{4,12},{8,0},{12,4},{16,24},{20,28},{24,16},{28,20},{1,9},{5... | collective-permute-start | bytes 10760 | tf_op jit(solution)/shard_map/ppermute | solution.py:81
  294.7 11.8 %collective-permute-start.10 = (bf16[2,2,2,48,1152]{4,3,2,1,0:T(8,128)(2,1)}, bf16[2,2,2,48,1152]{4,3,2,1,0:T(8,128)(2,1)}, u32[]{:S(2)}, u32[]{:S(2)}) collective-permute-start(bf16[2,2,2,48,1152]{4,3,2,1,0:T(8,128)(2,1)} %fusion.72), channel_id=1, source_target_pairs={{0,1},{1,0},{2,3},{3,2},{4,5},{5,4},{6,7},{7,6},{8,9},{9,8},{10,11... | collective-permute-start | bytes 2654216 | tf_op jit(solution)/shard_map/ppermute | solution.py:81
  296.8 5.6 %collective-permute-start.9 = (f32[896]{0:T(1024)S(1)}, f32[896]{0:T(1024)S(1)}, u32[]{:S(2)}, u32[]{:S(2)}) collective-permute-start(f32[896]{0:T(1024)S(1)} %add.177), channel_id=1, source_target_pairs={{0,16},{4,20},{8,24},{12,28},{16,0},{20,4},{24,8},{28,12},{1,17},{... | collective-permute-start | bytes 10760 | tf_op jit(solution)/shard_map/ppermute | solution.py:81
  305.0 14.4 %collective-permute-start.25 = (bf16[96,768]{1,0:T(8,128)(2,1)S(1)}, bf16[96,768]{1,0:T(8,128)(2,1)S(1)}, u32[]{:S(2)}, u32[]{:S(2)}) collective-permute-start(bf16[96,768]{1,0:T(8,128)(2,1)S(1)} %fusion.90), channel_id=1, source_target_pairs={{0,16},{4,20},{8,24},{12,28},{16,0},{20,4},{24,8},{28,12},{1,17},{... | collective-permute-start | bytes 442376 | tf_op jit(solution)/shard_map/ppermute | solution.py:81
  309.2 9.2 %collective-permute-start.11 = (bf16[2,2,48,1152]{3,2,1,0:T(8,128)(2,1)S(1)}, bf16[2,2,48,1152]{3,2,1,0:T(8,128)(2,1)S(1)}, u32[]{:S(2)}, u32[]{:S(2)}) collective-permute-start(bf16[2,2,48,1152]{3,2,1,0:T(8,128)(2,1)S(1)} %fusion.79), channel_id=1, source_target_pairs={{0,4},{4,0},{8,12},{12,8},{16,20},{20,16},{24,28},{28,24},{1,5},{5... | collective-permute-start | bytes 1327112 | tf_op jit(solution)/shard_map/ppermute | solution.py:81
  309.9 18.3 %collective-permute-start.21 = (bf16[96,768]{1,0:T(8,128)(2,1)S(1)}, bf16[96,768]{1,0:T(8,128)(2,1)S(1)}, u32[]{:S(2)}, u32[]{:S(2)}) collective-permute-start(bf16[96,768]{1,0:T(8,128)(2,1)S(1)} %fusion.89), channel_id=1, source_target_pairs={{0,16},{4,20},{8,24},{12,28},{16,0},{20,4},{24,8},{28,12},{1,17},{... | collective-permute-start | bytes 442376 | tf_op jit(solution)/shard_map/ppermute | solution.py:81
  318.5 6.0 %collective-permute-start.12 = (bf16[2,48,1152]{2,1,0:T(8,128)(2,1)S(1)}, bf16[2,48,1152]{2,1,0:T(8,128)(2,1)S(1)}, u32[]{:S(2)}, u32[]{:S(2)}) collective-permute-start(bf16[2,48,1152]{2,1,0:T(8,128)(2,1)S(1)} %fusion.87), channel_id=1, source_target_pairs={{0,8},{4,12},{8,0},{12,4},{16,24},{20,28},{24,16},{28,20},{1,9},{5... | collective-permute-start | bytes 663560 | tf_op jit(solution)/shard_map/ppermute | solution.py:81
  324.6 7.1 %collective-permute-start.13 = (bf16[48,1152]{1,0:T(8,128)(2,1)S(1)}, bf16[48,1152]{1,0:T(8,128)(2,1)S(1)}, u32[]{:S(2)}, u32[]{:S(2)}) collective-permute-start(bf16[48,1152]{1,0:T(8,128)(2,1)S(1)} %fusion.93), channel_id=1, source_target_pairs={{0,16},{4,20},{8,24},{12,28},{16,0},{20,4},{24,8},{28,12},{1,17},{... | collective-permute-start | bytes 331784 | tf_op jit(solution)/shard_map/ppermute | solution.py:81
  (46 other events, 255.8 us)
